TPU v7x, 128 devices: a whole 4x4x4 slice. The times are simulated.
128 devices in a mesh: dp: 4 (over x), tensor: 32 (over y, z, core).
Axes of the slice: x: 4, y: 4, z: 4, core: 2. Of those that a mesh axis runs over, the one named last changes fastest.
Arguments:
- tokens: bfloat16 [16384, 2048], P(('dp', 'tensor')), may hold values from -6 to 6
- norm_gain: bfloat16 [2048], replicated, may hold values from 0.099609375 to 1.8984375
- routes: int32 [16384, 6], P(('dp', 'tensor')), may hold values from 0 to 31, all different within a row; in each aligned block of 128 rows (0 to 127, 128 to 255, ...) at most 32 rows name the same one
- route_gates: bfloat16 [16384, 6], P(('dp', 'tensor')), may hold values from 0.19921875 to 1
- lengths: int32 [24], replicated, may hold values from 1 to 1920, 16384 in all
- request_adapter: int32 [24], replicated, may hold values from 0 to 31
- adapter_slot: int32 [32], replicated, may hold values from 0 to 31, each once
- expert_gate: bfloat16 [32, 2048, 1408], P('tensor'), may hold values from -0.125 to 0.125
- expert_up: bfloat16 [32, 2048, 1408], P('tensor'), may hold values from -0.125 to 0.125
- expert_down: bfloat16 [32, 1408, 2048], P('tensor'), may hold values from -0.15625 to 0.15625
- shared_gate: bfloat16 [2048, 1408], P(None, 'dp'), may hold values from -0.125 to 0.125
- shared_up_weight: bfloat16 [2048, 1408], P(None, 'dp'), may hold values from -0.125 to 0.125
- shared_down: bfloat16 [1408, 2048], P('dp'), may hold values from -0.15625 to 0.15625
- adapter_down: bfloat16 [32, 2048, 16], P('dp'), may hold values from -0.125 to 0.125
- adapter_up: bfloat16 [32, 16, 2048], P('dp'), may hold values from -1.5 to 1.5
- head_weight: bfloat16 [2048, 65536], P(None, ('dp', 'tensor')), may hold values from -0.375 to 0.375
Outputs:
- sublayer_out: bfloat16 [16384, 2048], P(('dp', 'tensor'))
- last_norm: float32 [24], replicated
- block_logit: float32 [24, 32], P(None, 'tensor')
Inputs may be any that keep to these rules, and one draw needn't show every extreme that they name: `routes`: in each aligned block of 128 rows (the rows of one device), no expert is named by more than 32 rows, a bound that some block reaches. The lengths sum to 16384; the largest is exactly 1920. Each position of the store appears once: adapter a is stored at position adapter_slot[a] of adapter_down and adapter_up.
All inputs are finite; a program needn't handle non-finite values.
Results may differ from a plain program's by a relative error of at most 0.0066.
Values may be sent and summed in bfloat16 or wider, within the bound.
A program may use at most 128 MiB of HBM per device.

v0:
```python
import jax
import jax.numpy as jnp
from jax import lax
from jax.sharding import PartitionSpec as P

CAP = 32


def apply_norm(tokens, norm_gain):
    values = tokens.astype(jnp.float32)
    scaled = lax.rsqrt(jnp.mean(values * values, axis=-1, keepdims=True) + 1e-06)
    return (values * scaled * norm_gain.astype(jnp.float32)).astype(jnp.bfloat16)


def feed_forward(inputs, gate_mat, up_mat, down_mat):
    gate_portion = jnp.dot(inputs, gate_mat, preferred_element_type=jnp.float32)
    up_part = jnp.dot(inputs, up_mat, preferred_element_type=jnp.float32)
    hidden = (jax.nn.silu(gate_portion) * up_part).astype(jnp.bfloat16)
    return jnp.dot(hidden, down_mat, preferred_element_type=jnp.float32)


def token_slots(positions, lengths, request_adapter, adapter_slot):
    request_ends = jnp.cumsum(lengths)
    request = jnp.sum((request_ends[None, :] <= positions[:, None]).astype(jnp.int32), axis=1)
    request_pick = (
        request[:, None] == jnp.arange(request_adapter.shape[0], dtype=jnp.int32)[None, :]
    )
    adapter = jnp.sum(jnp.where(request_pick, request_adapter[None, :], 0), axis=1)
    adapter_pick = adapter[:, None] == jnp.arange(adapter_slot.shape[0], dtype=jnp.int32)[None, :]
    return jnp.sum(jnp.where(adapter_pick, adapter_slot[None, :], 0), axis=1)


def adapter_delta(inputs, slot_ids, down_store, up_store):
    held_count = down_store.shape[0]
    model_width = down_store.shape[1]
    rank_size = down_store.shape[2]
    flat_down = jnp.transpose(down_store, (1, 0, 2)).reshape(model_width, held_count * rank_size)
    low_rank = jnp.dot(inputs, flat_down, preferred_element_type=jnp.float32)
    low_rank = low_rank.reshape(inputs.shape[0], held_count, rank_size)
    keep_mask = slot_ids[:, None] == jnp.arange(held_count, dtype=jnp.int32)[None, :]
    low_rank = jnp.where(keep_mask[:, :, None], low_rank, 0.0).astype(jnp.bfloat16)
    low_rank = low_rank.reshape(inputs.shape[0], held_count * rank_size)
    flat_up = up_store.reshape(held_count * rank_size, up_store.shape[2])
    return jnp.dot(low_rank, flat_up, preferred_element_type=jnp.float32)


def local(
    tokens,
    norm_gain,
    routes,
    route_gates,
    lengths,
    request_adapter,
    adapter_slot,
    expert_gate,
    expert_up,
    expert_down,
    shared_gate,
    shared_up_weight,
    shared_down,
    adapter_down,
    adapter_up,
    head_weight,
):
    tok_rows = tokens.shape[0]
    model_width = tokens.shape[1]
    route_count = routes.shape[1]
    tensor_size = lax.axis_size("tensor")
    tensor_pos = lax.axis_index("tensor")
    data_pos = lax.axis_index("dp")
    local_experts = expert_gate.shape[0]
    all_experts = local_experts * tensor_size
    slot_range = jnp.arange(CAP, dtype=jnp.int32)
    normed = apply_norm(tokens, norm_gain)
    numbers = jnp.arange(all_experts, dtype=jnp.int32)
    route_hits = routes[:, :, None] == numbers[None, None, :]
    chosen = jnp.any(route_hits, axis=1)
    weight = jnp.sum(
        jnp.where(route_hits, route_gates[:, :, None], jnp.zeros((), jnp.bfloat16)), axis=1
    )
    slot_place = jnp.cumsum(chosen.astype(jnp.int32), axis=0) - 1
    pooled, pooled_routes = (
        lax.all_gather(normed, "tensor", axis=0, tiled=True),
        lax.all_gather(routes.astype(jnp.bfloat16), "tensor", axis=0, tiled=True),
    )
    pooled = pooled.reshape(tensor_size, tok_rows, model_width)
    source_routes = pooled_routes.astype(jnp.int32).reshape(tensor_size, tok_rows, route_count)
    own_numbers = tensor_pos * local_experts + jnp.arange(local_experts, dtype=jnp.int32)
    source_hits = source_routes[:, :, :, None] == own_numbers[None, None, None, :]
    source_chosen = jnp.any(source_hits, axis=2)
    source_place = jnp.cumsum(source_chosen.astype(jnp.int32), axis=1) - 1
    source_pick = source_chosen[:, :, :, None] & (
        source_place[:, :, :, None] == slot_range[None, None, None, :]
    )
    source_pick = jnp.where(source_pick, 1.0, 0.0).astype(jnp.bfloat16)
    incoming = jnp.einsum(
        "sijc,sid->sjcd", source_pick, pooled, preferred_element_type=jnp.float32
    ).astype(jnp.bfloat16)
    gate_portion = jnp.einsum(
        "secd,edf->secf", incoming, expert_gate, preferred_element_type=jnp.float32
    )
    up_part = jnp.einsum("secd,edf->secf", incoming, expert_up, preferred_element_type=jnp.float32)
    hidden = (jax.nn.silu(gate_portion) * up_part).astype(jnp.bfloat16)
    expert_out = jnp.einsum(
        "secf,efd->secd", hidden, expert_down, preferred_element_type=jnp.float32
    ).astype(jnp.bfloat16)
    returned_rows = lax.all_to_all(expert_out, "tensor", split_axis=0, concat_axis=0, tiled=True)
    returned_rows = returned_rows.reshape(all_experts, CAP, model_width)
    mixing_result = jnp.where(
        slot_place[:, :, None] == slot_range[None, None, :],
        weight[:, :, None],
        jnp.zeros((), jnp.bfloat16),
    )
    routed_output = jnp.einsum(
        "kbt,btw->kw", mixing_result, returned_rows, preferred_element_type=jnp.float32
    )
    own_base = (data_pos * tensor_size + tensor_pos) * tok_rows
    own_positions = own_base + jnp.arange(tok_rows, dtype=jnp.int32)
    peer_rows = lax.all_gather(normed, "dp", axis=0, tiled=True)
    shared_sum = lax.psum_scatter(
        feed_forward(peer_rows, shared_gate, shared_up_weight, shared_down),
        "dp",
        scatter_dimension=0,
        tiled=True,
    )
    own_slots = token_slots(own_positions, lengths, request_adapter, adapter_slot)
    store_down, store_up = (
        lax.all_gather(adapter_down, "dp", axis=0, tiled=True),
        lax.all_gather(adapter_up, "dp", axis=0, tiled=True),
    )
    summed = routed_output + shared_sum + adapter_delta(normed, own_slots, store_down, store_up)
    sublayer_out = summed.astype(jnp.bfloat16)
    request_ends = jnp.cumsum(lengths)
    last_pick = jnp.where(request_ends[:, None] - 1 == own_positions[None, :], 1.0, 0.0).astype(
        jnp.bfloat16
    )
    last_part = jnp.dot(last_pick, sublayer_out, preferred_element_type=jnp.float32)
    last_states = lax.psum(last_part, ("dp", "tensor"))
    last_norm = jnp.sqrt(jnp.sum(last_states * last_states, axis=1))
    logits = jnp.dot(
        last_states.astype(jnp.bfloat16), head_weight, preferred_element_type=jnp.float32
    )
    block_logit = lax.pmax(jnp.max(logits, axis=1), "dp")
    return (sublayer_out, last_norm, block_logit[:, None])


def solution(mesh):
    placed = (
        P(("dp", "tensor"), None),
        P(),
        P(("dp", "tensor"), None),
        P(("dp", "tensor"), None),
        P(),
        P(),
        P(),
        P("tensor", None, None),
        P("tensor", None, None),
        P("tensor", None, None),
        P(None, "dp"),
        P(None, "dp"),
        P("dp", None),
        P("dp", None, None),
        P("dp", None, None),
        P(None, ("dp", "tensor")),
    )
    return jax.shard_map(
        local,
        mesh=mesh,
        in_specs=placed,
        out_specs=(P(("dp", "tensor"), None), P(), P(None, "tensor")),
        check_vma=False,
    )
```

profile of v0, /device:TPU:0, one launch (start us, length us, event | category | flops | bytes accessed | tf_op | source)
XLA Modules:
  0.0 401.9 jit_solution(9235097486257809376)
XLA Ops:
  7.2 0.9 convert_element_type.84
  8.1 1.3 fusion.41
  9.4 2.0 fusion.43
  12.3 32.6 %all-gather.7.cloned.1.call-done = bf16[512,2048]{1,0:T(8,128)(2,1)} async-done(((bf16[128,2048]{1,0:T(8,128)(2,1)}), bf16[512,2048]{1,0:T(8,128)(2,1)}) %all-gather.7.cloned.1.call-update) | async-done | bytes 2097168 | tf_op jit(solution)/shard_map/all_gather | solution.py:119
  44.9 3.8 fusion.82
  48.7 6.3 %fusion.32 = f32[512,2048]{1,0:T(8,128)} fusion(bf16[352,2048]{1,0:T(8,128)(2,1)S(1)} %copy-done.8, bf16[512,2048]{1,0:T(8,128)(2,1)} %all-gather.7.cloned.1.call-done, bf16[2048,352]{0,1:T(8,128)(2,1)} %param.27, f32[512,352]{0,1:T(8,128)} %fusion.82), kind=kOutput, calls=%fused_computation.29 | convolution fusion | flops 1477476352 | bytes 9895936 | tf_op jit(solution)/shard_map/dot_general | solution.py:19
  55.1 1.0 copy-done.4
  56.0 1.1 copy.47
  57.2 24.6 %all_gather.15 = bf16[4096,6]{0,1:T(8,128)(2,1)S(1)} all-gather(bf16[128,6]{0,1:T(8,128)(2,1)S(1)} %convert_element_type.79), channel_id=1, replica_groups=mesh['dp'=4,'tensor'=32] {'tensor'}, dimensions={0}, use_global_device_ids=true | all-gather | bytes 50688 | tf_op jit(solution)/shard_map/all_gather | solution.py:84
  82.1 38.3 %all-gather.5.cloned.1.call-done = bf16[4096,2048]{1,0:T(8,128)(2,1)} async-done(((bf16[128,2048]{1,0:T(8,128)(2,1)}), bf16[4096,2048]{1,0:T(8,128)(2,1)}) %all-gather.5.cloned.1.call-update) | async-done | bytes 16777232 | tf_op jit(solution)/shard_map/all_gather | solution.py:83
  120.4 8.1 %convolution_convert_fusion = bf16[32,32,2048]{2,1,0:T(8,128)(2,1)S(1)} fusion(bf16[32,128,2048]{2,1,0:T(8,128)(2,1)} %bitcast.109, s32[32,128]{1,0:T(8,128)S(1)} %broadcast_add_fusion.1, pred[32,128]{1,0:T(8,128)(4,1)S(1)} %bitcast.111), kind=kOutput, calls=%fused_computation.16 | convolution fusion | flops 539492352 | bytes 20992000 | tf_op jit(solution)/shard_map/sijc,sid->sjcd/dot_general | solution.py:96
  128.5 2.1 copy-done.1
  130.6 10.7 %fusion.3 = f32[32,32,1408]{2,1,0:T(8,128)} fusion(bf16[32,32,2048]{2,1,0:T(8,128)(2,1)S(1)} %convolution_convert_fusion, bf16[1,2048,1408]{2,1,0:T(8,128)(2,1)} %param.24), kind=kOutput, calls=%fused_computation.4 | convolution fusion | flops 5905580032 | bytes 15728640 | tf_op jit(solution)/shard_map/secd,edf->secf/dot_general | solution.py:102
  141.3 21.0 %convert_bitcast_fusion = bf16[32,1,32,2048]{3,2,1,0:T(8,128)(2,1)} fusion(bf16[1,1408,2048]{2,1,0:T(8,128)(2,1)} %param.25, f32[32,32,1408]{2,1,0:T(8,128)} %fusion.3, bf16[32,32,2048]{2,1,0:T(8,128)(2,1)} %copy-done.1, bf16[1,2048,1408]{2,1,0:T(8,128)(2,1)} %param.23), kind=kOutput, calls=%fused_computation.15 | convolution fusion | flops 11821907968 | bytes 25690112 | tf_op jit(solution)/shard_map/secf,efd->secd/dot_general | solution.py:104
  162.4 5.2 %all-to-all-start = ((bf16[32,1,32,2048]{3,2,1,0:T(8,128)(2,1)}), bf16[32,1,32,2048]{3,2,1,0:T(8,128)(2,1)}, u32[]{:S(2)}, u32[]{:S(2)}) async-start(bf16[32,1,32,2048]{3,2,1,0:T(8,128)(2,1)} %convert_bitcast_fusion), calls=%async_computation | async-start | bytes 8388608 | tf_op jit(solution)/shard_map/all_to_all | solution.py:107
  169.5 50.9 %all-to-all-done = bf16[32,1,32,2048]{3,2,1,0:T(8,128)(2,1)} async-done(((bf16[32,1,32,2048]{3,2,1,0:T(8,128)(2,1)}), bf16[32,1,32,2048]{3,2,1,0:T(8,128)(2,1)}, u32[]{:S(2)}, u32[]{:S(2)}) %all-to-all-start) | async-done | bytes 4194336 | tf_op jit(solution)/shard_map/all_to_all | solution.py:107
  220.4 4.3 %fusion.23 = f32[128,2048]{1,0:T(8,128)} fusion(f32[128,2048]{1,0:T(8,128)} %reduce-scatter.2.cloned.1.call-done, bf16[32,1,32,2048]{3,2,1,0:T(8,128)(2,1)} %all-to-all-done, s32[128,32]{0,1:T(8,128)S(1)} %copy.43, bf16[128,32]{0,1:T(8,128)(2,1)S(1)} %fusion.68), kind=kOutput, calls=%fused_computation.21 | convolution fusion | flops 537395200 | bytes 6316032 | tf_op jit(solution)/shard_map/kbt,btw->kw/dot_general | solution.py:114
  224.7 9.1 %all-gather.9.cloned.1.call-done = bf16[32,2048,16]{1,2,0:T(8,128)(2,1)} async-done(((bf16[8,2048,16]{1,2,0:T(8,128)(2,1)}), bf16[32,2048,16]{1,2,0:T(8,128)(2,1)}) %all-gather.9.cloned.1.call-update) | async-done | bytes 2097168 | tf_op jit(solution)/shard_map/all_gather | solution.py:128
  233.7 4.5 %fusion.26 = bf16[128,2048]{1,0:T(8,128)(2,1)S(1)} fusion(f32[128,2048]{1,0:T(8,128)} %fusion.23, bf16[32,16,2048]{2,0,1:T(8,128)(2,1)} %all-gather.11.cloned.1.call-done, bf16[32,16,2048]{2,1,0:T(8,128)(2,1)} %bitcast.110, bf16[128,2048]{1,0:T(8,128)(2,1)S(1)} %copy-done.2, pred[128,32]{0,1:T(8,128)(4,1)S(1)} %iota_compare_fusion.3), kind=kOutput, calls=%fused_computation.22 | convolution fusion | flops 537526272 | bytes 6295552 | tf_op jit(solution)/shard_map/dot_general | solution.py:44
  238.3 0.9 fusion.69
  239.2 143.1 %all-reduce.2.cloned.1.call-done = f32[24,2048]{1,0:T(8,128)} async-done(((f32[24,2048]{1,0:T(8,128)}), f32[24,2048]{1,0:T(8,128)}) %all-reduce.2.cloned.1.call-update) | async-done | bytes 196624 | tf_op jit(solution)/shard_map/psum | solution.py:138
  382.3 1.4 convolution_reduce_fusion
  383.7 9.7 %pmax.7 = f32[24,1]{0,1:T(1,128)} all-reduce(f32[24,1]{0,1:T(1,128)S(1)} %bitcast.112), channel_id=1, replica_groups=mesh['dp'=4,'tensor'=32] {'dp'}, use_global_device_ids=true, to_apply=%region_14.15 | all-reduce | flops 24 | bytes 192 | tf_op jit(solution)/shard_map/pmax | solution.py:143
  393.5 1.1 multiply_reduce_fusion
  (57 shorter events, 3.7 us)
Async XLA Ops:
  7.2 375.2 %copy-start = (bf16[2048,512]{1,0:T(8,128)(2,1)S(1)}, bf16[2048,512]{1,0:T(8,128)(2,1)}, u32[]{:S(2)}) copy-start(bf16[2048,512]{1,0:T(8,128)(2,1)} %param.31) | copy-start | bytes 6291460
  7.2 41.5 %copy-start.8 = (bf16[352,2048]{1,0:T(8,128)(2,1)S(1)}, bf16[352,2048]{1,0:T(8,128)(2,1)}, u32[]{:S(2)}) copy-start(bf16[352,2048]{1,0:T(8,128)(2,1)} %param.28) | copy-start | bytes 4325380
  7.2 37.7 %all-gather.7.cloned.1.call-start = ((), (), s32[]{:S(2)}) async-start(), calls=%async_computation.3 | async-start | bytes 2621440 | tf_op jit(solution)/shard_map/all_gather | solution.py:119
  11.5 109.0 %all-gather.5.cloned.1.call-start = ((), (), s32[]{:S(2)}) async-start(), calls=%async_computation.2 | async-start | bytes 17301504 | tf_op jit(solution)/shard_map/all_gather | solution.py:83
  12.2 157.3 %reduce-scatter.2.cloned.1.call-start = ((), (), s32[]{:S(2)}) async-start(), calls=%async_computation.4 | async-start | bytes 5242880 | tf_op jit(solution)/shard_map/reduce_scatter | solution.py:120
  55.0 1.0 copy-start.4
  55.0 2.1 copy-start.5
  55.0 169.6 %all-gather.11.cloned.1.call-start = ((), (), s32[]{:S(2)}) async-start(), calls=%async_computation.6 | async-start | bytes 2621440 | tf_op jit(solution)/shard_map/all_gather | solution.py:129
  128.5 2.1 copy-start.1
  162.3 6.5 %copy-start.7 = (s32[24]{0:T(128)S(1)}, s32[24]{0:T(128)}, u32[]{:S(2)}) copy-start(s32[24]{0:T(128)} %param.20) | copy-start | bytes 292
  162.3 6.9 %copy-start.9 = (s32[24]{0:T(128)S(1)}, s32[24]{0:T(128)}, u32[]{:S(2)}) copy-start(s32[24]{0:T(128)} %param.21) | copy-start | bytes 292
  162.3 7.0 %copy-start.10 = (s32[32]{0:T(128)S(1)}, s32[32]{0:T(128)}, u32[]{:S(2)}) copy-start(s32[32]{0:T(128)} %param.22) | copy-start | bytes 388
  162.4 7.1 %copy-start.6 = (bf16[128,6]{0,1:T(8,128)(2,1)S(1)}, bf16[128,6]{0,1:T(8,128)(2,1)}, u32[]{:S(2)}) copy-start(bf16[128,6]{0,1:T(8,128)(2,1)} %param.19) | copy-start | bytes 4612
  162.4 58.0 %all-to-all-start = ((bf16[32,1,32,2048]{3,2,1,0:T(8,128)(2,1)}), bf16[32,1,32,2048]{3,2,1,0:T(8,128)(2,1)}, u32[]{:S(2)}, u32[]{:S(2)}) async-start(bf16[32,1,32,2048]{3,2,1,0:T(8,128)(2,1)} %convert_bitcast_fusion), calls=%async_computation | async-start | bytes 8388608 | tf_op jit(solution)/shard_map/all_to_all | solution.py:107
  167.6 66.1 %copy-start.2 = (bf16[128,2048]{1,0:T(8,128)(2,1)S(1)}, bf16[128,2048]{1,0:T(8,128)(2,1)}, u32[]{:S(2)}) copy-start(bf16[128,2048]{1,0:T(8,128)(2,1)} %fusion.43) | copy-start | bytes 1572868
  167.6 66.1 %all-gather.9.cloned.1.call-start = ((), (), s32[]{:S(2)}) async-start(), calls=%async_computation.5 | async-start | bytes 2621440 | tf_op jit(solution)/shard_map/all_gather | solution.py:128
  168.2 214.1 %all-reduce.2.cloned.1.call-start = ((), (), s32[]{:S(2)}) async-start(), calls=%async_computation.7 | async-start | bytes 393216 | tf_op jit(solution)/shard_map/psum | solution.py:138
  238.3 156.8 %copy-start.3 = (bf16[128,2048]{1,0:T(8,128)(2,1)}, bf16[128,2048]{1,0:T(8,128)(2,1)S(1)}, u32[]{:S(2)}) copy-start(bf16[128,2048]{1,0:T(8,128)(2,1)S(1)} %fusion.26) | copy-start | bytes 1572868
Sparse Core Ops, SparseCore 0:
  11.6 33.2 all-gather.6
  47.7 72.6 all-gather.4
  122.8 46.1 reduce-scatter.1
  170.7 30.5 all-gather.10
  202.9 30.8 all-gather.8
  239.3 142.9 all-reduce.1
where the time goes:
time: 402 us
  waiting for transfers between devices  275 us (68%)
  matrix products  61.1 us (15%)
  blocking collectives  34.3 us (9%)
  between operations  14.3 us (4%)
  other arithmetic  6.28 us (2%)
  starting transfers between devices  5.69 us (1%)
  local copies, waits for them, and re-layouts  4.94 us (1%)
    psum x1, waiting for transfers between devices, local(): last_states = lax.psum(last_part, ('dp', 'tensor'))  143 us
    all_to_all x1, waiting for transfers between devices, local(): lax.all_to_all(expert_out, 'tensor', split_axis=0, concat_axis=0, tiled=T...  50.9 us
    all_gather x1, waiting for transfers between devices, local(): lax.all_gather(normed, 'tensor', axis=0, tiled=True)  38.3 us
    all_gather x1, waiting for transfers between devices, local(): peer_rows = lax.all_gather(normed, 'dp', axis=0, tiled=True)  32.6 us
    all_gather x1, blocking collectives, local(): lax.all_gather(routes.astype(jnp.bfloat16), 'tensor', axis=0, tiled=True)  24.6 us
    dot_general x1, matrix products, local(): jnp.einsum('secf,efd->secd', hidden, expert_down, preferred_element_type=...  21 us
    dot_general x1, matrix products, local(): jnp.einsum('secd,edf->secf', incoming, expert_up, preferred_element_type=...  10.7 us
    pmax x1, blocking collectives, local(): block_logit = lax.pmax(jnp.max(logits, axis=1), 'dp')  9.75 us
  transfers between devices with their start and end apart: 7, of which 5 were waited for; matrix products, arithmetic and copies ran while one was open for 14% of the time, Pallas kernels for 0%

commit v1 on v0

--- a/solution.py
+++ b/solution.py
@@ -4,6 +4,24 @@
 from jax.sharding import PartitionSpec as P
 
 CAP = 32
+
+
+def ring_gather(array, axis, dim):
+    ways, here, step = (lax.axis_size(axis), lax.axis_index(axis), array.shape[dim])
+    shape = [n * ways if d == dim else n for d, n in enumerate(array.shape)]
+    full = lax.dynamic_update_slice_in_dim(
+        jnp.zeros(shape, array.dtype), array, here * step, axis=dim
+    )
+    going_up = going_down = array
+    for far in range(1, ways // 2 + 1):
+        going_up = lax.ppermute(going_up, axis, [(d, (d + 1) % ways) for d in range(ways)])
+        full = lax.dynamic_update_slice_in_dim(full, going_up, (here - far) % ways * step, axis=dim)
+        if 2 * far < ways:
+            going_down = lax.ppermute(going_down, axis, [(d, (d - 1) % ways) for d in range(ways)])
+            full = lax.dynamic_update_slice_in_dim(
+                full, going_down, (here + far) % ways * step, axis=dim
+            )
+    return full
 
 
 def apply_norm(tokens, norm_gain):
@@ -125,7 +143,7 @@
     )
     own_slots = token_slots(own_positions, lengths, request_adapter, adapter_slot)
     store_down, store_up = (
-        lax.all_gather(adapter_down, "dp", axis=0, tiled=True),
+        ring_gather(adapter_down, "dp", 0),
         lax.all_gather(adapter_up, "dp", axis=0, tiled=True),
     )
     summed = routed_output + shared_sum + adapter_delta(normed, own_slots, store_down, store_up)

time: 402 us -> 394 us (0.980)
  waiting for transfers between devices: 275 us -> 257 us
  local copies, waits for them, and re-layouts: 4.94 us -> 11.8 us
    all_to_all x1, waiting for transfers between devices: 50.9 us -> 3.64 us  [local(): lax.all_to_all(expert_out, 'tensor', split_axis=0, concat_axis=0, tiled=T...]
    ppermute x0 -> x3, waiting for transfers between devices: none -> 36.9 us  [the longest x2 36.9 us: ring_gather(): lax.ppermute(going_up, axis, [(d, (d + 1) % ways) for d in range(ways)])]
    all_gather x1 -> x0, waiting for transfers between devices: 9.08 us -> none  [local(): lax.all_gather(adapter_down, 'dp', axis=0, tiled=True)]
    dynamic_update_slice x0 -> x4, local copies, waits for them, and re-layouts: none -> 5.53 us  [the longest x2 3.83 us: ring_gather(): lax.dynamic_update_slice_in_dim(full, going_up, (here - far) % ways * ste...]
  transfers between devices with their start and end apart: 7 -> 9, of which waited for: 5 -> 6; matrix products, arithmetic and copies ran while one was open for 14% -> 16% of each run, Pallas kernels for 0% -> 0%
where the time goes in v1:
time: 394 us; the launch traced here: 393 us
  waiting for transfers between devices  257 us (65%)
  matrix products  61 us (15%)
  blocking collectives  34.3 us (9%)
  between operations  14 us (4%)
  local copies, waits for them, and re-layouts  11.8 us (3%)
  starting transfers between devices  8.19 us (2%)
  other arithmetic  6.19 us (2%)
    psum x1, waiting for transfers between devices, local(): last_states = lax.psum(last_part, ('dp', 'tensor'))  144 us
    all_gather x1, waiting for transfers between devices, local(): lax.all_gather(normed, 'tensor', axis=0, tiled=True)  39.9 us
    ppermute x2, waiting for transfers between devices, ring_gather(): lax.ppermute(going_up, axis, [(d, (d + 1) % ways) for d in range(ways)])  36.9 us
    all_gather x1, waiting for transfers between devices, local(): peer_rows = lax.all_gather(normed, 'dp', axis=0, tiled=True)  32.6 us
    all_gather x1, blocking collectives, local(): lax.all_gather(routes.astype(jnp.bfloat16), 'tensor', axis=0, tiled=True)  24.5 us
    dot_general x1, matrix products, local(): jnp.einsum('secf,efd->secd', hidden, expert_down, preferred_element_type=...  21 us
    dot_general x1, matrix products, local(): jnp.einsum('secd,edf->secf', incoming, expert_up, preferred_element_type=...  10.8 us
    pmax x1, blocking collectives, local(): block_logit = lax.pmax(jnp.max(logits, axis=1), 'dp')  9.75 us
  transfers between devices with their start and end apart: 9, of which 6 were waited for; matrix products, arithmetic and copies ran while one was open for 16% of the time, Pallas kernels for 0%

profile of v1, /device:TPU:0, one launch (start us, length us, event | category | flops | bytes accessed | tf_op | source)
XLA Modules:
  0.0 393.0 jit_solution(1857679917461303422)
XLA Ops:
  7.2 1.4 fusion.41
  9.3 2.0 fusion.43
  12.2 32.6 %all-gather.6.cloned.1.call-done = bf16[512,2048]{1,0:T(8,128)(2,1)} async-done(((bf16[128,2048]{1,0:T(8,128)(2,1)}), bf16[512,2048]{1,0:T(8,128)(2,1)}) %all-gather.6.cloned.1.call-update) | async-done | bytes 2097168 | tf_op jit(solution)/shard_map/all_gather | solution.py:137
  44.8 3.8 fusion.82
  48.6 6.3 %fusion.32 = f32[512,2048]{1,0:T(8,128)} fusion(bf16[352,2048]{1,0:T(8,128)(2,1)S(1)} %copy-done.9, bf16[512,2048]{1,0:T(8,128)(2,1)} %all-gather.6.cloned.1.call-done, bf16[2048,352]{0,1:T(8,128)(2,1)} %param.27, f32[512,352]{0,1:T(8,128)} %fusion.82), kind=kOutput, calls=%fused_computation.29 | convolution fusion | flops 1477476352 | bytes 9895936 | tf_op jit(solution)/shard_map/dot_general | solution.py:37
  55.6 24.5 %all_gather.12 = bf16[4096,6]{0,1:T(8,128)(2,1)S(1)} all-gather(bf16[128,6]{0,1:T(8,128)(2,1)S(1)} %convert_element_type.79), channel_id=1, replica_groups=mesh['dp'=4,'tensor'=32] {'tensor'}, dimensions={0}, use_global_device_ids=true | all-gather | bytes 50688 | tf_op jit(solution)/shard_map/all_gather | solution.py:102
  80.5 39.9 %all-gather.4.cloned.1.call-done = bf16[4096,2048]{1,0:T(8,128)(2,1)} async-done(((bf16[128,2048]{1,0:T(8,128)(2,1)}), bf16[4096,2048]{1,0:T(8,128)(2,1)}) %all-gather.4.cloned.1.call-update) | async-done | bytes 16777232 | tf_op jit(solution)/shard_map/all_gather | solution.py:101
  120.4 8.1 %convolution_convert_fusion = bf16[32,32,2048]{2,1,0:T(8,128)(2,1)S(1)} fusion(bf16[32,128,2048]{2,1,0:T(8,128)(2,1)} %bitcast.109, s32[32,128]{1,0:T(8,128)S(1)} %broadcast_add_fusion.1, pred[32,128]{1,0:T(8,128)(4,1)S(1)} %bitcast.110), kind=kOutput, calls=%fused_computation.16 | convolution fusion | flops 539492352 | bytes 20992000 | tf_op jit(solution)/shard_map/sijc,sid->sjcd/dot_general | solution.py:114
  128.5 2.1 copy-done.1
  130.6 10.8 %fusion.3 = f32[32,32,1408]{2,1,0:T(8,128)} fusion(bf16[32,32,2048]{2,1,0:T(8,128)(2,1)S(1)} %convolution_convert_fusion, bf16[1,2048,1408]{2,1,0:T(8,128)(2,1)} %param.24), kind=kOutput, calls=%fused_computation.4 | convolution fusion | flops 5905580032 | bytes 15728640 | tf_op jit(solution)/shard_map/secd,edf->secf/dot_general | solution.py:120
  141.4 21.0 %convert_bitcast_fusion = bf16[32,1,32,2048]{3,2,1,0:T(8,128)(2,1)} fusion(bf16[1,1408,2048]{2,1,0:T(8,128)(2,1)} %param.25, f32[32,32,1408]{2,1,0:T(8,128)} %fusion.3, bf16[32,32,2048]{2,1,0:T(8,128)(2,1)} %copy-done.1, bf16[1,2048,1408]{2,1,0:T(8,128)(2,1)} %param.23), kind=kOutput, calls=%fused_computation.15 | convolution fusion | flops 11821907968 | bytes 25690112 | tf_op jit(solution)/shard_map/secf,efd->secd/dot_general | solution.py:122
  162.4 5.2 %all-to-all-start = ((bf16[32,1,32,2048]{3,2,1,0:T(8,128)(2,1)}), bf16[32,1,32,2048]{3,2,1,0:T(8,128)(2,1)}, u32[]{:S(2)}, u32[]{:S(2)}) async-start(bf16[32,1,32,2048]{3,2,1,0:T(8,128)(2,1)} %convert_bitcast_fusion), calls=%async_computation | async-start | bytes 8388608 | tf_op jit(solution)/shard_map/all_to_all | solution.py:125
  168.9 2.8 collective-permute-start.1
  172.5 1.6 broadcast_in_dim.117
  175.0 14.4 %collective-permute-done = bf16[8,2048,16]{1,2,0:T(8,128)(2,1)} collective-permute-done((bf16[8,2048,16]{1,2,0:T(8,128)(2,1)S(1)}, bf16[8,2048,16]{1,2,0:T(8,128)(2,1)}, u32[]{:S(2)}, u32[]{:S(2)}) %collective-permute-start) | collective-permute-done | bytes 524320 | tf_op jit(solution)/shard_map/ppermute | solution.py:17
  189.5 1.9 constant_dynamic-update-slice_fusion.1
  192.3 22.5 %collective-permute-done.2 = bf16[8,2048,16]{1,2,0:T(8,128)(2,1)} collective-permute-done((bf16[8,2048,16]{1,2,0:T(8,128)(2,1)}, bf16[8,2048,16]{1,2,0:T(8,128)(2,1)}, u32[]{:S(2)}, u32[]{:S(2)}) %collective-permute-start.2) | collective-permute-done | bytes 524320 | tf_op jit(solution)/shard_map/ppermute | solution.py:17
  214.8 1.9 constant_dynamic-update-slice_fusion.3
  216.8 3.6 all-to-all-done
  220.4 4.2 %fusion.23 = f32[128,2048]{1,0:T(8,128)} fusion(f32[128,2048]{1,0:T(8,128)} %reduce-scatter.2.cloned.1.call-done, bf16[32,1,32,2048]{3,2,1,0:T(8,128)(2,1)} %all-to-all-done, s32[128,32]{0,1:T(8,128)S(1)} %copy.43, bf16[128,32]{0,1:T(8,128)(2,1)S(1)} %fusion.68), kind=kOutput, calls=%fused_computation.21 | convolution fusion | flops 537395200 | bytes 6316032 | tf_op jit(solution)/shard_map/kbt,btw->kw/dot_general | solution.py:132
  224.6 4.5 %fusion.26 = bf16[128,2048]{1,0:T(8,128)(2,1)S(1)} fusion(f32[128,2048]{1,0:T(8,128)} %fusion.23, bf16[32,16,2048]{2,0,1:T(8,128)(2,1)} %all-gather.8.cloned.1.call-done, bf16[32,16,2048]{2,1,0:T(8,128)(2,1)} %bitcast.28, bf16[128,2048]{1,0:T(8,128)(2,1)S(1)} %copy-done.2, pred[128,32]{0,1:T(8,128)(4,1)S(1)} %iota_compare_fusion.3), kind=kOutput, calls=%fused_computation.22 | convolution fusion | flops 537526272 | bytes 6295552 | tf_op jit(solution)/shard_map/dot_general | solution.py:62
  230.1 143.6 %all-reduce.2.cloned.1.call-done = f32[24,2048]{1,0:T(8,128)} async-done(((f32[24,2048]{1,0:T(8,128)}), f32[24,2048]{1,0:T(8,128)}) %all-reduce.2.cloned.1.call-update) | async-done | bytes 196624 | tf_op jit(solution)/shard_map/psum | solution.py:156
  375.3 1.4 convolution_reduce_fusion
  376.7 9.7 %pmax.7 = f32[24,1]{0,1:T(1,128)} all-reduce(f32[24,1]{0,1:T(1,128)S(1)} %bitcast.111), channel_id=1, replica_groups=mesh['dp'=4,'tensor'=32] {'dp'}, use_global_device_ids=true, to_apply=%region_14.15 | all-reduce | flops 24 | bytes 192 | tf_op jit(solution)/shard_map/pmax | solution.py:161
  (67 shorter events, 9.0 us)
Async XLA Ops:
  7.2 368.1 %copy-start = (bf16[2048,512]{1,0:T(8,128)(2,1)S(1)}, bf16[2048,512]{1,0:T(8,128)(2,1)}, u32[]{:S(2)}) copy-start(bf16[2048,512]{1,0:T(8,128)(2,1)} %param.31) | copy-start | bytes 6291460
  7.2 37.6 %all-gather.6.cloned.1.call-start = ((), (), s32[]{:S(2)}) async-start(), calls=%async_computation.3 | async-start | bytes 2621440 | tf_op jit(solution)/shard_map/all_gather | solution.py:137
  11.3 37.2 %copy-start.9 = (bf16[352,2048]{1,0:T(8,128)(2,1)S(1)}, bf16[352,2048]{1,0:T(8,128)(2,1)}, u32[]{:S(2)}) copy-start(bf16[352,2048]{1,0:T(8,128)(2,1)} %param.28) | copy-start | bytes 4325380
  11.4 109.1 %all-gather.4.cloned.1.call-start = ((), (), s32[]{:S(2)}) async-start(), calls=%async_computation.2 | async-start | bytes 17301504 | tf_op jit(solution)/shard_map/all_gather | solution.py:101
  12.1 204.7 %reduce-scatter.2.cloned.1.call-start = ((), (), s32[]{:S(2)}) async-start(), calls=%async_computation.4 | async-start | bytes 5242880 | tf_op jit(solution)/shard_map/reduce_scatter | solution.py:138
  54.9 0.7 copy-start.6
  128.5 2.1 copy-start.1
  162.4 5.3 %copy-start.4 = (bf16[8,16,2048]{2,1,0:T(8,128)(2,1)S(1)}, bf16[8,16,2048]{2,1,0:T(8,128)(2,1)}, u32[]{:S(2)}) copy-start(bf16[8,16,2048]{2,1,0:T(8,128)(2,1)} %param.30) | copy-start | bytes 1572868
  162.4 6.5 %copy-start.5 = (bf16[8,2048,16]{1,2,0:T(8,128)(2,1)S(1)}, bf16[8,2048,16]{1,2,0:T(8,128)(2,1)}, u32[]{:S(2)}) copy-start(bf16[8,2048,16]{1,2,0:T(8,128)(2,1)} %param.29) | copy-start | bytes 1572868
  162.4 9.3 %copy-start.8 = (s32[24]{0:T(128)S(1)}, s32[24]{0:T(128)}, u32[]{:S(2)}) copy-start(s32[24]{0:T(128)} %param.20) | copy-start | bytes 292
  162.4 9.9 %copy-start.10 = (s32[24]{0:T(128)S(1)}, s32[24]{0:T(128)}, u32[]{:S(2)}) copy-start(s32[24]{0:T(128)} %param.21) | copy-start | bytes 292
  162.4 10.0 %copy-start.11 = (s32[32]{0:T(128)S(1)}, s32[32]{0:T(128)}, u32[]{:S(2)}) copy-start(s32[32]{0:T(128)} %param.22) | copy-start | bytes 388
  162.4 58.0 %all-to-all-start = ((bf16[32,1,32,2048]{3,2,1,0:T(8,128)(2,1)}), bf16[32,1,32,2048]{3,2,1,0:T(8,128)(2,1)}, u32[]{:S(2)}, u32[]{:S(2)}) async-start(bf16[32,1,32,2048]{3,2,1,0:T(8,128)(2,1)} %convert_bitcast_fusion), calls=%async_computation | async-start | bytes 8388608 | tf_op jit(solution)/shard_map/all_to_all | solution.py:125
  167.6 21.8 %copy-start.7 = (bf16[128,6]{0,1:T(8,128)(2,1)S(1)}, bf16[128,6]{0,1:T(8,128)(2,1)}, u32[]{:S(2)}) copy-start(bf16[128,6]{0,1:T(8,128)(2,1)} %param.19) | copy-start | bytes 4612
  167.6 57.0 %all-gather.8.cloned.1.call-start = ((), (), s32[]{:S(2)}) async-start(), calls=%async_computation.5 | async-start | bytes 2621440 | tf_op jit(solution)/shard_map/all_gather | solution.py:147
  168.8 204.9 %all-reduce.2.cloned.1.call-start = ((), (), s32[]{:S(2)}) async-start(), calls=%async_computation.6 | async-start | bytes 393216 | tf_op jit(solution)/shard_map/psum | solution.py:156
  168.9 22.5 %collective-permute-start.1 = (bf16[8,2048,16]{1,2,0:T(8,128)(2,1)S(1)}, bf16[8,2048,16]{1,2,0:T(8,128)(2,1)S(1)}, u32[]{:S(2)}, u32[]{:S(2)}) collective-permute-start(bf16[8,2048,16]{1,2,0:T(8,128)(2,1)S(1)} %copy-done.5), channel_id=1, source_target_pairs={{0,96},{32,0},{64,32},{96,64},{1,97},{33,1},{65,33},{97,65},{2,98}... | collective-permute-start | bytes 1572872 | tf_op jit(solution)/shard_map/ppermute | solution.py:20
  171.7 17.7 %collective-permute-start = (bf16[8,2048,16]{1,2,0:T(8,128)(2,1)S(1)}, bf16[8,2048,16]{1,2,0:T(8,128)(2,1)}, u32[]{:S(2)}, u32[]{:S(2)}) collective-permute-start(bf16[8,2048,16]{1,2,0:T(8,128)(2,1)S(1)} %copy-done.5), channel_id=1, source_target_pairs={{0,32},{32,64},{64,96},{96,0},{1,33},{33,65},{65,97},{97,1},{2,34}... | collective-permute-start | bytes 1572872 | tf_op jit(solution)/shard_map/ppermute | solution.py:17
  189.4 25.4 %collective-permute-start.2 = (bf16[8,2048,16]{1,2,0:T(8,128)(2,1)}, bf16[8,2048,16]{1,2,0:T(8,128)(2,1)}, u32[]{:S(2)}, u32[]{:S(2)}) collective-permute-start(bf16[8,2048,16]{1,2,0:T(8,128)(2,1)} %collective-permute-done), channel_id=1, source_target_pairs={{0,32},{32,64},{64,96},{96,0},{1,33},{33,65},{65,97},{97,1},{2,34}... | collective-permute-start | bytes 1572872 | tf_op jit(solution)/shard_map/ppermute | solution.py:17
  216.8 7.9 %copy-start.2 = (bf16[128,2048]{1,0:T(8,128)(2,1)S(1)}, bf16[128,2048]{1,0:T(8,128)(2,1)}, u32[]{:S(2)}) copy-start(bf16[128,2048]{1,0:T(8,128)(2,1)} %fusion.43) | copy-start | bytes 1572868
  229.1 157.3 %copy-start.3 = (bf16[128,2048]{1,0:T(8,128)(2,1)}, bf16[128,2048]{1,0:T(8,128)(2,1)S(1)}, u32[]{:S(2)}) copy-start(bf16[128,2048]{1,0:T(8,128)(2,1)S(1)} %fusion.26) | copy-start | bytes 1572868
Sparse Core Ops, SparseCore 0:
  11.5 33.2 all-gather.5
  47.6 72.7 all-gather.3
  122.8 46.2 reduce-scatter.1
  170.7 43.9 all-gather.7
  230.2 143.4 all-reduce.1
